TPU v7x, 256 devices: a whole 4x4x8 slice. The times are simulated.
256 devices in a mesh: wall: 2 (over z_lo), plane: 128 (over x, y, z_hi, core).
Axes of the slice: x: 4, y: 4, z: 8 (z_hi: 4, z_lo: 2; z = z_hi * 2 + z_lo), core: 2. Of those that a mesh axis runs over, the one named last changes fastest.
Arguments:
- jacobian: float32 [3, 16, 16, 32, 128, 128], P(None, None, None, 'wall', 'plane'), as said below
- residual: float32 [16, 32, 128, 128], P(None, 'wall', 'plane')
- previous_update: float32 [16, 32, 128, 128], P(None, 'wall', 'plane'), may hold values from -6 to 6
- offline_coupling: float32 [4, 16, 32, 128, 128], P(None, None, 'wall', 'plane'), may hold values from 0.003 to 0.03
- wake_partner: int32 [128, 128], P('plane'), may hold values from 0 to 127, each once within a row
- line_length: int32 [128, 128], P('plane'), may hold values from 16 to 32
- bottom_flag: int32 [128, 128], P('plane'), may hold values 0 or 1
Outputs:
- update: float32 [16, 32, 128, 128], P(None, 'wall', 'plane')
Inputs may be any that keep to these rules, and one draw needn't show every extreme that they name: jacobian[2, :, :, k] is the transpose of jacobian[0, :, :, k + 1], every jacobian[1, :, :, k] is symmetric, and every row of a line's matrix is strictly diagonally dominant with a positive diagonal. `bottom_flag`: 1 where a column's first cell lies on the wake cut, 0 where it lies on the capsule wall. `wake_partner`: for a wake-cut column (i, j), the spanwise index of the column at station (i + 64) modulo 128, on the other branch of the cut, that lies beneath its first cell; each row is a permutation of 0 to 127.
All inputs are finite; a program needn't handle non-finite values. No bound on the sum of `bottom_flag` on one device may be relied on, other than what follows from the above.
Results may differ from a plain program's by a relative error of at most 0.0003.
Values sent between devices are 32-bit elements; how exact they have to be, the bound alone decides.
No kernel may reach another device: no remote copies, remote signals or barrier semaphores. Data moves between devices by JAX's collectives and lax.ppermute only.
A program may use at most 192 MiB of HBM per device.

v0:
```python
import jax
import jax.numpy as jnp
from jax import lax
from jax.sharding import PartitionSpec as P

precise = lax.Precision.HIGHEST


def with_halo(block, sides, width):
    for axis, dim in sides:
        count = lax.axis_size(axis)
        forward = [(i, i + 1) for i in range(count - 1)]
        backward = [(target, source) for source, target in forward]
        low = lax.ppermute(
            lax.slice_in_dim(block, block.shape[dim] - width, None, axis=dim), axis, forward
        )
        high = lax.ppermute(lax.slice_in_dim(block, 0, width, axis=dim), axis, backward)
        block = jnp.concatenate([low, block, high], axis=dim)
    return block


def from_behind(block, axis, distance):
    devices = range(lax.axis_size(axis))
    route = [(i - distance, i) for i in devices if i - distance in devices]
    return lax.ppermute(block, axis, route)


def product(left, right):
    return jnp.einsum("vwc,wuc->vuc", left, right, precision=precise)


def solve_block(matrix, given):
    extent = matrix.shape[0]
    augmented = jnp.concatenate([matrix, given], axis=1)
    for pivot in range(extent):
        pivot_row = augmented[pivot] / augmented[pivot, pivot][None, :]
        augmented = augmented - augmented[:, pivot][:, None, :] * pivot_row[None]
        augmented = augmented.at[pivot].set(pivot_row)
    return augmented[:, extent:]


def effective(lower, middle, upper, active_here, active_above, not_bottom):
    identity = jnp.eye(lower.shape[0], dtype=jnp.float32)[:, :, None, None]
    return (
        lower * (active_here * not_bottom)[None, None],
        middle * active_here[None, None] + identity * (1.0 - active_here)[None, None],
        upper * active_above[None, None],
    )


def eliminate(lower, middle, upper, source, block_in, vector_in, levels):
    extent = lower.shape[0]
    blocks = jnp.zeros(lower.shape, jnp.float32)
    vectors = jnp.zeros(source.shape, jnp.float32)

    def advance(level, state):
        block_prev, vector_prev, blocks, vectors = state
        below = lax.dynamic_index_in_dim(lower, level, 2, keepdims=False)
        centre = lax.dynamic_index_in_dim(middle, level, 2, keepdims=False)
        above = lax.dynamic_index_in_dim(upper, level, 2, keepdims=False)
        given = lax.dynamic_index_in_dim(source, level, 2, keepdims=False)
        schur = centre - product(below, block_prev)
        reduced = given - product(below, vector_prev)
        joined = solve_block(schur, jnp.concatenate([above, reduced], axis=1))
        block_next = joined[:, :extent]
        vector_next = joined[:, extent:]
        blocks = lax.dynamic_update_index_in_dim(blocks, block_next, level, 2)
        vectors = lax.dynamic_update_index_in_dim(vectors, vector_next, level, 2)
        return (block_next, vector_next, blocks, vectors)

    return lax.fori_loop(0, levels, advance, (block_in, vector_in, blocks, vectors))


def substitute(blocks, vectors, value_above, levels, result):

    def retreat(count, state):
        value_next, result = state
        level = levels - 1 - count
        block = lax.dynamic_index_in_dim(blocks, level, 2, keepdims=False)
        vector = lax.dynamic_index_in_dim(vectors, level, 2, keepdims=False)
        value = vector - product(block, value_next)
        result = lax.dynamic_update_index_in_dim(result, value, level, 2)
        return (value, result)

    return lax.fori_loop(0, levels, retreat, (value_above, result))


def per_device(
    jacobian, residual, previous_update, offline_coupling, wake_partner, line_length, bottom_flag
):
    unknowns = jacobian.shape[1]
    depth = jacobian.shape[3]
    stations = jacobian.shape[4]
    span = jacobian.shape[5]
    columns = stations * span
    wall_index = lax.axis_index("wall")
    plane_index = lax.axis_index("plane")
    planes = lax.axis_size("plane")
    padded = with_halo(previous_update, (("plane", 2),), 1)
    offline = (
        offline_coupling[0] * padded[:, :, :-2]
        + offline_coupling[1] * padded[:, :, 2:]
        + offline_coupling[2] * jnp.roll(previous_update, 1, axis=3)
        + offline_coupling[3] * jnp.roll(previous_update, -1, axis=3)
    )
    bottom_row = previous_update[:, 0]
    mirror_index = (plane_index + planes // 2) % planes
    whole = lax.all_gather(bottom_row, "plane", axis=1, tiled=True)
    facing = lax.dynamic_slice_in_dim(whole, mirror_index * stations, stations, 1)
    partner = jnp.take_along_axis(facing, wake_partner[None], axis=2)
    weight = bottom_flag.astype(jnp.float32) * (wall_index == 0).astype(jnp.float32)
    wake = (
        jnp.einsum("vwij,wij->vij", jacobian[0, :, :, 0], partner, precision=precise) * weight[None]
    )
    levels = wall_index * depth + jnp.arange(depth, dtype=jnp.int32)
    active = (levels[:, None, None] < line_length[None]).astype(jnp.float32)
    active_above = ((levels + 1)[:, None, None] < line_length[None]).astype(jnp.float32)
    not_bottom = (levels > 0).astype(jnp.float32)[:, None]
    source = residual + offline
    source = source.at[:, 0].add(-wake)
    source = (source * active[None]).reshape(unknowns, 1, depth, columns)
    blocks = jacobian.reshape(3, unknowns, unknowns, depth, columns)
    lower, middle, upper = effective(
        blocks[0],
        blocks[1],
        blocks[2],
        active.reshape(depth, columns),
        active_above.reshape(depth, columns),
        not_bottom,
    )
    empty_block = jnp.zeros((unknowns, unknowns, columns), jnp.float32)
    empty_vector = jnp.zeros((unknowns, 1, columns), jnp.float32)
    block_in = empty_block
    vector_in = empty_vector
    parts = eliminate(lower, middle, upper, source, block_in, vector_in, depth)
    handed = from_behind(
        jnp.concatenate([parts[2][:, :, depth - 1], parts[3][:, :, depth - 1]], axis=1), "wall", 1
    )
    block_in = handed[:, :unknowns]
    vector_in = handed[:, unknowns:]
    parts = eliminate(lower, middle, upper, source, block_in, vector_in, depth)
    value_above = empty_vector
    solved = substitute(
        parts[2], parts[3], value_above, depth, jnp.zeros(source.shape, jnp.float32)
    )
    value_above = from_behind(solved[1][:, :, 0], "wall", -1)
    solution = substitute(
        parts[2], parts[3], value_above, depth, jnp.zeros(source.shape, jnp.float32)
    )[1]
    return solution[:, 0].reshape(unknowns, depth, stations, span)


def solution(mesh):
    return jax.shard_map(
        per_device,
        mesh=mesh,
        in_specs=(
            P(None, None, None, "wall", "plane", None),
            P(None, "wall", "plane", None),
            P(None, "wall", "plane", None),
            P(None, None, "wall", "plane", None),
            P("plane", None),
            P("plane", None),
            P("plane", None),
        ),
        out_specs=P(None, "wall", "plane", None),
        check_vma=False,
    )
```

profile of v0, /device:TPU:1, one launch (start us, length us, event | category | flops | bytes accessed | tf_op | source)
XLA Modules:
  0.0 605.0 jit_solution(280235571044377390)
XLA Ops:
  7.5 6.3 %collective-permute-start = (f32[16,16,1,128]{3,0,1,2:T(8,128)S(1)}, f32[16,16,1,128]{3,0,1,2:T(8,128)S(1)}, u32[]{:S(2)}, u32[]{:S(2)}) collective-permute-start(f32[16,16,1,128]{3,0,1,2:T(8,128)S(1)} %copy.131), channel_id=1, source_target_pairs={{0,1},{1,2},{2,3},{3,4},{4,5},{5,6},{6,7},{7,8},{8,9},{9,10},{10,1... | collective-permute-start | bytes 393224 | tf_op jit(solution)/shard_map/ppermute | solution.py:14
  22.3 8.3 %fusion.22 = (f32[1,16,16,16,1,128]{5,4,3,2,1,0:T(1,128)}, f32[1,16,16,16,1,128]{5,4,3,2,1,0:T(1,128)}, f32[1,16,16,16,1,128]{5,4,3,2,1,0:T(1,128)S(1)}) fusion(f32[3,16,16,16,1,128]{5,4,3,2,1,0:T(1,128)} %param.81), kind=kLoop, calls=%fused_computation.232 | loop fusion | bytes 12582912 | tf_op jit(solution)/shard_map/slice | solution.py:126
  30.6 12.0 %copy.215 = f32[1,16,16,16,1,128]{2,1,5,3,4,0:T(8,128)} copy(f32[1,16,16,16,1,128]{5,4,3,2,1,0:T(1,128)} %get-tuple-element.1768) | data formatting | bytes 4194304
  42.6 10.7 %copy.216 = f32[1,16,16,16,1,128]{2,1,5,3,4,0:T(8,128)} copy(f32[1,16,16,16,1,128]{5,4,3,2,1,0:T(1,128)S(1)} %get-tuple-element.1769) | data formatting | bytes 4194304
  57.6 15.1 %fusion.10 = f32[16,16,16,128]{1,0,3,2:T(8,128)} fusion(f32[1,16,16,16,1,128]{2,1,5,3,4,0:T(8,128)} %copy.215, f32[16,128]{1,0:T(8,128)S(1)} %copy-done.3, f32[16,16]{1,0:T(8,128)S(1)} %fusion.20, f32[16,128]{1,0:T(8,128)S(1)} %get-tuple-element.1781), kind=kLoop, calls=%fused_computation.191 | loop fusion | flops 1572864 | bytes 4211712 | tf_op jit(solution)/shard_map/add | solution.py:46
  72.8 6.5 %bitcast_multiply_fusion.2 = f32[16,16,16,128]{1,0,3,2:T(8,128)} fusion(f32[1,16,16,16,1,128]{2,1,5,3,4,0:T(8,128)S(1)} %bitcast.632, f32[16,128]{1,0:T(8,128)S(1)} %copy-done.2), kind=kLoop, calls=%fused_computation.189 | loop fusion | flops 524288 | bytes 4202496 | tf_op jit(solution)/shard_map/mul | solution.py:45
  80.5 23.8 %all-gather.3.cloned.1.call-done = f32[16,128,1,128]{3,2,1,0:T(1,128)} async-done(((f32[16,1,1,128]{3,2,1,0:T(1,128)}), f32[16,128,1,128]{3,2,1,0:T(1,128)}) %all-gather.3.cloned.1.call-update) | async-done | bytes 1048592 | tf_op jit(solution)/shard_map/all_gather | solution.py:108
  106.0 185.2 %while.112 = (s32[]{:T(128)}, f32[16,16,128]{2,0,1:T(8,128)S(1)}, f32[16,1,128]{2,0,1:T(8,128)S(1)}, f32[16,16,16,128]{3,0,1,2:T(8,128)}, f32[16,1,16,128]{3,0,2...) while((s32[]{:T(128)}, f32[16,16,128]{2,0,1:T(8,128)S(1)}, ...), condition=%wide.region_1.2_spmd, body=%wide.region_0.1_spmd.sunk | while | flops 8890370 | bytes 15271725 | solution.py:71
  296.7 249.2 %while.113 = (s32[]{:T(128)}, f32[16,16,128]{2,0,1:T(8,128)S(1)}, f32[16,1,128]{2,0,1:T(8,128)S(1)}, f32[16,16,16,128]{3,2,1,0:T(8,128)}, f32[16,1,16,128]{3,0,2...) while((s32[]{:T(128)}, f32[16,16,128]{2,0,1:T(8,128)S(1)}, ...), condition=%wide.region_3.4_spmd, body=%wide.region_2.3_spmd.sunk | while | flops 8890370 | bytes 15926577 | solution.py:71
  338.8 4.5 dynamic_update_slice.80
  354.4 4.5 dynamic_update_slice.80
  369.9 4.5 dynamic_update_slice.80
  385.5 4.5 dynamic_update_slice.80
  401.0 4.5 dynamic_update_slice.80
  432.2 4.5 dynamic_update_slice.80
  447.8 4.5 dynamic_update_slice.80
  463.4 4.5 dynamic_update_slice.80
  479.0 4.5 dynamic_update_slice.80
  494.6 4.5 dynamic_update_slice.80
  510.2 4.5 dynamic_update_slice.80
  525.8 4.5 dynamic_update_slice.80
  541.4 4.5 dynamic_update_slice.80
  545.9 23.7 %while.115 = (s32[]{:T(128)}, f32[16,1,128]{2,0,1:T(8,128)S(1)}, f32[16,1,16,128]{3,2,1,0:T(8,128)S(1)}, f32[16,1,16,128]{3,0,2,1:T(8,128)S(1)}, f32[16,16,16,12...) while((s32[]{:T(128)}, f32[16,1,128]{2,0,1:T(8,128)S(1)}, ...), condition=%wide.region_5.6_spmd.clone, body=%wide.region_4.5_spmd.clone.sunk | while | flops 67591 | bytes 467105 | solution.py:85
  574.1 23.4 %while.114 = (s32[]{:T(128)}, f32[16,1,128]{2,0,1:T(8,128)S(1)}, f32[16,1,16,128]{3,2,1,0:T(8,128)S(1)}, f32[16,1,16,128]{3,0,2,1:T(8,128)S(1)}, f32[16,16,16,12...) while((s32[]{:T(128)}, f32[16,1,128]{2,0,1:T(8,128)S(1)}, ...), condition=%wide.region_7.8_spmd, body=%wide.region_6.7_spmd.sunk | while | flops 65542 | bytes 450711 | solution.py:85
  (3677 shorter events, 426.8 us)
Async XLA Ops:
  6.5 14.4 %copy-start.4 = (s32[1,128]{1,0:T(1,128)S(1)}, s32[1,128]{1,0:T(1,128)}, u32[]{:S(2)}) copy-start(s32[1,128]{1,0:T(1,128)} %param.86) | copy-start | bytes 1540
  6.5 97.8 %all-gather.3.cloned.1.call-start = ((), (), s32[]{:S(2)}) async-start(), calls=%async_computation | async-start | bytes 1056768 | tf_op jit(solution)/shard_map/all_gather | solution.py:108
  7.5 72.7 %collective-permute-start = (f32[16,16,1,128]{3,0,1,2:T(8,128)S(1)}, f32[16,16,1,128]{3,0,1,2:T(8,128)S(1)}, u32[]{:S(2)}, u32[]{:S(2)}) collective-permute-start(f32[16,16,1,128]{3,0,1,2:T(8,128)S(1)} %copy.131), channel_id=1, source_target_pairs={{0,1},{1,2},{2,3},{3,4},{4,5},{5,6},{6,7},{7,8},{8,9},{9,10},{10,1... | collective-permute-start | bytes 393224 | tf_op jit(solution)/shard_map/ppermute | solution.py:14
  13.8 66.4 %collective-permute-start.1 = (f32[16,16,1,128]{3,0,1,2:T(8,128)S(1)}, f32[16,16,1,128]{3,0,1,2:T(8,128)S(1)}, u32[]{:S(2)}, u32[]{:S(2)}) collective-permute-start(f32[16,16,1,128]{3,0,1,2:T(8,128)S(1)} %copy.131), channel_id=1, source_target_pairs={{1,0},{2,1},{3,2},{4,3},{5,4},{6,5},{7,6},{8,7},{9,8},{10,9},{11,1... | collective-permute-start | bytes 393224 | tf_op jit(solution)/shard_map/ppermute | solution.py:17
  53.3 4.3 copy-start.3
  53.3 19.4 %slice-start = ((s8[16777216]{0:T(1024)(128)(4,1)}), s8[4194304]{0:T(1024)(128)(4,1)S(1)}, s32[]{:S(2)}) async-start(s8[16777216]{0:T(1024)(128)(4,1)} %bitcast.631), calls=%async_computation.1 | async-start | bytes 8388608
  57.6 15.1 %slice-start.1 = ((s8[16777216]{0:T(1024)(128)(4,1)}), s8[4194304]{0:T(1024)(128)(4,1)S(1)}, s32[]{:S(2)}) async-start(s8[16777216]{0:T(1024)(128)(4,1)} %bitcast.631), calls=%async_computation.2 | async-start | bytes 8388608
  57.6 15.1 %slice-start.2 = ((s8[16777216]{0:T(1024)(128)(4,1)}), s8[4194304]{0:T(1024)(128)(4,1)S(1)}, s32[]{:S(2)}) async-start(s8[16777216]{0:T(1024)(128)(4,1)} %bitcast.631), calls=%async_computation.3 | async-start | bytes 8388608
  57.6 15.1 %slice-start.3 = ((s8[16777216]{0:T(1024)(128)(4,1)}), s8[4194304]{0:T(1024)(128)(4,1)S(1)}, s32[]{:S(2)}) async-start(s8[16777216]{0:T(1024)(128)(4,1)} %bitcast.631), calls=%async_computation.4 | async-start | bytes 8388608
  57.6 15.1 %copy-start.2 = (f32[16,128]{1,0:T(8,128)S(1)}, f32[16,128]{1,0:T(8,128)}, u32[]{:S(2)}) copy-start(f32[16,128]{1,0:T(8,128)} %get-tuple-element.1778) | copy-start | bytes 24580
  72.7 6.5 %copy-start.7 = (s32[1,128]{1,0:T(1,128)S(1)}, s32[1,128]{1,0:T(1,128)}, u32[]{:S(2)}) copy-start(s32[1,128]{1,0:T(1,128)} %param.87) | copy-start | bytes 1540
  72.8 7.4 %copy-start.6 = (s32[128]{0:T(128)S(1)}, s32[128]{0:T(128)}, u32[]{:S(2)}) copy-start(s32[128]{0:T(128)} %fusion.21) | copy-start | bytes 1540
  72.8 7.5 %copy-start = (f32[16,16,1,128]{3,2,1,0:T(1,128)S(1)}, f32[16,16,1,128]{3,2,1,0:T(1,128)}, u32[]{:S(2)}) copy-start(f32[16,16,1,128]{3,2,1,0:T(1,128)} %param.82) | copy-start | bytes 393220
  72.8 33.0 %copy-start.5 = (pred[128]{0:T(512)(128)(4,1)S(1)}, pred[128]{0:T(512)(128)(4,1)}, u32[]{:S(2)}) copy-start(pred[128]{0:T(512)(128)(4,1)} %compare_and_fusion) | copy-start | bytes 388
  292.2 4.4 collective-permute-start.2
  569.6 4.5 collective-permute-start.3
  597.5 0.7 copy-start.1
Sparse Core Ops, SparseCore 0:
  17.2 87.0 all-gather.2
where the time goes:
time: 611 us; the launch traced here: 605 us
  local copies, waits for them, and re-layouts  330 us (54%)
  other arithmetic  110 us (18%)
  matrix products  86.9 us (14%)
  waiting for transfers between devices  30 us (5%)
  loops' own time  23.4 us (4%)
  between operations  13.8 us (2%)
  starting transfers between devices  11 us (2%)
    dot_general x32, matrix products, product(): return jnp.einsum('vwc,wuc->vuc', left, right, precision=precise)  86.9 us
    dynamic_update_slice x48, local copies, waits for them, and re-layouts, advance(): blocks = lax.dynamic_update_index_in_dim(blocks, block_next, level, 2)  84.7 us
    while x48, other arithmetic  50.4 us
    scatter x512, local copies, waits for them, and re-layouts, solve_block(): augmented = augmented.at[pivot].set(pivot_row)  44.3 us
    dynamic_slice x32, local copies, waits for them, and re-layouts, retreat(): block = lax.dynamic_index_in_dim(blocks, level, 2, keepdims=False)  42.4 us
    slice x32, local copies, waits for them, and re-layouts, solve_block(): pivot_row = augmented[pivot] / augmented[pivot, pivot][None, :]  32.9 us
    squeeze x32, local copies, waits for them, and re-layouts, advance(): above = lax.dynamic_index_in_dim(upper, level, 2, keepdims=False)  29.3 us
    unnamed x28, local copies, waits for them, and re-layouts  24.4 us
  transfers between devices with their start and end apart: 5, of which 3 were waited for; matrix products, arithmetic and copies ran while one was open for 11% of the time, Pallas kernels for 0%

commit v1 on v0

--- a/solution.py
+++ b/solution.py
@@ -105,7 +105,9 @@
     )
     bottom_row = previous_update[:, 0]
     mirror_index = (plane_index + planes // 2) % planes
-    whole = lax.all_gather(bottom_row, "plane", axis=1, tiled=True)
+    whole = jnp.concatenate(
+        lax.all_to_all(jnp.stack([bottom_row] * lax.axis_size("plane")), "plane", 0, 0), axis=1
+    )
     facing = lax.dynamic_slice_in_dim(whole, mirror_index * stations, stations, 1)
     partner = jnp.take_along_axis(facing, wake_partner[None], axis=2)
     weight = bottom_flag.astype(jnp.float32) * (wall_index == 0).astype(jnp.float32)

time: 611 us -> 592 us (0.969)
  waiting for transfers between devices: 30 us -> 5.08 us
  starting transfers between devices: 11 us -> 28.3 us
  between operations: 13.8 us -> 0.5 us
    all_gather x1 -> x0, waiting for transfers between devices: 23.8 us -> none  [per_device(): whole = lax.all_gather(bottom_row, 'plane', axis=1, tiled=True)]
    all_to_all x0 -> x1, starting transfers between devices: none -> 16 us  [per_device(): lax.all_to_all(jnp.stack([bottom_row] * lax.axis_size('plane')), 'plane',...]
    another operation x36 -> x39, local copies, waits for them, and re-layouts: 16.9 us -> 18.1 us
    unnamed x28 -> x44, local copies, waits for them, and re-layouts: 24.4 us -> 24.5 us
  transfers between devices with their start and end apart: 5 -> 5, of which waited for: 3 -> 2; matrix products, arithmetic and copies ran while one was open for 11% -> 11% of each run, Pallas kernels for 0% -> 0%
where the time goes in v1:
time: 592 us; the launch traced here: 584 us
  local copies, waits for them, and re-layouts  330 us (56%)
  other arithmetic  110 us (19%)
  matrix products  87 us (15%)
  starting transfers between devices  28.3 us (5%)
  loops' own time  23.4 us (4%)
    dot_general x32, matrix products, product(): return jnp.einsum('vwc,wuc->vuc', left, right, precision=precise)  87 us
    dynamic_update_slice x48, local copies, waits for them, and re-layouts, advance(): blocks = lax.dynamic_update_index_in_dim(blocks, block_next, level, 2)  84.8 us
    while x48, other arithmetic  50.4 us
    scatter x512, local copies, waits for them, and re-layouts, solve_block(): augmented = augmented.at[pivot].set(pivot_row)  44.3 us
    dynamic_slice x32, local copies, waits for them, and re-layouts, retreat(): block = lax.dynamic_index_in_dim(blocks, level, 2, keepdims=False)  42.4 us
    slice x32, local copies, waits for them, and re-layouts, solve_block(): pivot_row = augmented[pivot] / augmented[pivot, pivot][None, :]  32.9 us
    squeeze x32, local copies, waits for them, and re-layouts, advance(): above = lax.dynamic_index_in_dim(upper, level, 2, keepdims=False)  29.3 us
    unnamed x44, local copies, waits for them, and re-layouts  24.5 us
  transfers between devices with their start and end apart: 5, of which 2 were waited for; matrix products, arithmetic and copies ran while one was open for 11% of the time, Pallas kernels for 0%

profile of v1, /device:TPU:1, one launch (start us, length us, event | category | flops | bytes accessed | tf_op | source)
XLA Modules:
  0.0 584.1 jit_solution(3549836393480310353)
XLA Ops:
  1.0 6.3 %collective-permute-start = (f32[16,16,1,128]{3,0,1,2:T(8,128)S(1)}, f32[16,16,1,128]{3,0,1,2:T(8,128)}, u32[]{:S(2)}, u32[]{:S(2)}) collective-permute-start(f32[16,16,1,128]{3,0,1,2:T(8,128)S(1)} %copy.131), channel_id=1, source_target_pairs={{0,1},{1,2},{2,3},{3,4},{4,5},{5,6},{6,7},{7,8},{8,9},{9,10},{10,1... | collective-permute-start | bytes 393224 | tf_op jit(solution)/shard_map/ppermute | solution.py:14
  11.0 16.0 %all-to-all-start = ((f32[128,16,1,128]{3,1,2,0:T(8,128)}), f32[128,16,1,128]{3,1,2,0:T(8,128)S(1)}, u32[]{:S(2)}, u32[]{:S(2)}) async-start(f32[128,16,1,128]{3,1,2,0:T(8,128)} %stack.3), calls=%async_computation | async-start | bytes 2097152 | tf_op jit(solution)/shard_map/all_to_all | solution.py:109
  31.0 8.3 %fusion.22 = (f32[1,16,16,16,1,128]{5,4,3,2,1,0:T(1,128)}, f32[1,16,16,16,1,128]{5,4,3,2,1,0:T(1,128)}, f32[1,16,16,16,1,128]{5,4,3,2,1,0:T(1,128)S(1)}) fusion(f32[3,16,16,16,1,128]{5,4,3,2,1,0:T(1,128)} %param.81), kind=kLoop, calls=%fused_computation.232 | loop fusion | bytes 12582912 | tf_op jit(solution)/shard_map/slice | solution.py:128
  39.4 12.0 %copy.215 = f32[1,16,16,16,1,128]{2,1,5,3,4,0:T(8,128)} copy(f32[1,16,16,16,1,128]{5,4,3,2,1,0:T(1,128)} %get-tuple-element.1768) | data formatting | bytes 4194304
  51.4 10.7 %copy.216 = f32[1,16,16,16,1,128]{2,1,5,3,4,0:T(8,128)} copy(f32[1,16,16,16,1,128]{5,4,3,2,1,0:T(1,128)S(1)} %get-tuple-element.1769) | data formatting | bytes 4194304
  66.4 15.1 %fusion.10 = f32[16,16,16,128]{1,0,3,2:T(8,128)} fusion(f32[1,16,16,16,1,128]{2,1,5,3,4,0:T(8,128)} %copy.215, f32[16,128]{1,0:T(8,128)S(1)} %copy-done.10, f32[16,16]{1,0:T(8,128)S(1)} %fusion.20, f32[16,128]{1,0:T(8,128)S(1)} %get-tuple-element.1781), kind=kLoop, calls=%fused_computation.191 | loop fusion | flops 1572864 | bytes 4211712 | tf_op jit(solution)/shard_map/add | solution.py:46
  81.6 6.4 %bitcast_multiply_fusion.2 = f32[16,16,16,128]{1,0,3,2:T(8,128)} fusion(f32[1,16,16,16,1,128]{2,1,5,3,4,0:T(8,128)S(1)} %bitcast.633, f32[16,128]{1,0:T(8,128)S(1)} %copy-done.9), kind=kLoop, calls=%fused_computation.189 | loop fusion | flops 524288 | bytes 4202496 | tf_op jit(solution)/shard_map/mul | solution.py:45
  91.4 185.2 %while.112 = (s32[]{:T(128)}, f32[16,16,128]{2,0,1:T(8,128)S(1)}, f32[16,1,128]{2,0,1:T(8,128)S(1)}, f32[16,16,16,128]{3,0,1,2:T(8,128)}, f32[16,1,16,128]{3,0,2...) while((s32[]{:T(128)}, f32[16,16,128]{2,0,1:T(8,128)S(1)}, ...), condition=%wide.region_1.2_spmd, body=%wide.region_0.1_spmd.sunk | while | flops 8890370 | bytes 15271725 | solution.py:71
  282.3 249.5 %while.113 = (s32[]{:T(128)}, f32[16,16,128]{2,0,1:T(8,128)S(1)}, f32[16,1,128]{2,0,1:T(8,128)S(1)}, f32[16,16,16,128]{3,2,1,0:T(8,128)}, f32[16,1,16,128]{3,0,2...) while((s32[]{:T(128)}, f32[16,16,128]{2,0,1:T(8,128)S(1)}, ...), condition=%wide.region_3.4_spmd, body=%wide.region_2.3_spmd.sunk | while | flops 8890370 | bytes 15926577 | solution.py:71
  293.3 4.5 dynamic_update_slice.80
  324.5 4.5 dynamic_update_slice.80
  340.1 4.5 dynamic_update_slice.80
  355.7 4.5 dynamic_update_slice.80
  371.2 4.5 dynamic_update_slice.80
  418.1 4.5 dynamic_update_slice.80
  433.7 4.5 dynamic_update_slice.80
  449.3 4.5 dynamic_update_slice.80
  464.9 4.5 dynamic_update_slice.80
  480.5 4.5 dynamic_update_slice.80
  496.0 4.5 dynamic_update_slice.80
  511.6 4.5 dynamic_update_slice.80
  527.2 4.5 dynamic_update_slice.80
  531.8 23.7 %while.115 = (s32[]{:T(128)}, f32[16,1,128]{2,0,1:T(8,128)S(1)}, f32[16,1,16,128]{3,2,1,0:T(8,128)S(1)}, f32[16,1,16,128]{3,0,2,1:T(8,128)S(1)}, f32[16,16,16,12...) while((s32[]{:T(128)}, f32[16,1,128]{2,0,1:T(8,128)S(1)}, ...), condition=%wide.region_5.6_spmd.clone, body=%wide.region_4.5_spmd.clone.sunk | while | flops 67591 | bytes 467105 | solution.py:85
  560.0 23.4 %while.114 = (s32[]{:T(128)}, f32[16,1,128]{2,0,1:T(8,128)S(1)}, f32[16,1,16,128]{3,2,1,0:T(8,128)S(1)}, f32[16,1,16,128]{3,0,2,1:T(8,128)S(1)}, f32[16,16,16,12...) while((s32[]{:T(128)}, f32[16,1,128]{2,0,1:T(8,128)S(1)}, ...), condition=%wide.region_7.8_spmd, body=%wide.region_6.7_spmd.sunk | while | flops 65542 | bytes 450711 | solution.py:85
  (3693 shorter events, 426.9 us)
Async XLA Ops:
  0.0 27.0 %copy-start.14 = (s32[1,128]{1,0:T(1,128)S(1)}, s32[1,128]{1,0:T(1,128)}, u32[]{:S(2)}) copy-start(s32[1,128]{1,0:T(1,128)} %param.85) | copy-start | bytes 1540
  1.0 88.0 %collective-permute-start = (f32[16,16,1,128]{3,0,1,2:T(8,128)S(1)}, f32[16,16,1,128]{3,0,1,2:T(8,128)}, u32[]{:S(2)}, u32[]{:S(2)}) collective-permute-start(f32[16,16,1,128]{3,0,1,2:T(8,128)S(1)} %copy.131), channel_id=1, source_target_pairs={{0,1},{1,2},{2,3},{3,4},{4,5},{5,6},{6,7},{7,8},{8,9},{9,10},{10,1... | collective-permute-start | bytes 393224 | tf_op jit(solution)/shard_map/ppermute | solution.py:14
  7.3 81.7 %collective-permute-start.1 = (f32[16,16,1,128]{3,0,1,2:T(8,128)S(1)}, f32[16,16,1,128]{3,0,1,2:T(8,128)}, u32[]{:S(2)}, u32[]{:S(2)}) collective-permute-start(f32[16,16,1,128]{3,0,1,2:T(8,128)S(1)} %copy.131), channel_id=1, source_target_pairs={{1,0},{2,1},{3,2},{4,3},{5,4},{6,5},{7,6},{8,7},{9,8},{10,9},{11,1... | collective-permute-start | bytes 393224 | tf_op jit(solution)/shard_map/ppermute | solution.py:17
  9.9 19.0 %copy-start = (f32[4,16,16,1,128]{4,3,2,1,0:T(1,128)S(1)}, f32[4,16,16,1,128]{4,3,2,1,0:T(1,128)}, u32[]{:S(2)}) copy-start(f32[4,16,16,1,128]{4,3,2,1,0:T(1,128)} %param.84) | copy-start | bytes 1572868
  11.0 18.7 %copy-start.11 = (s32[1,128]{1,0:T(1,128)S(1)}, s32[1,128]{1,0:T(1,128)}, u32[]{:S(2)}) copy-start(s32[1,128]{1,0:T(1,128)} %param.86) | copy-start | bytes 1540
  11.0 79.4 %all-to-all-start = ((f32[128,16,1,128]{3,1,2,0:T(8,128)}), f32[128,16,1,128]{3,1,2,0:T(8,128)S(1)}, u32[]{:S(2)}, u32[]{:S(2)}) async-start(f32[128,16,1,128]{3,1,2,0:T(8,128)} %stack.3), calls=%async_computation | async-start | bytes 2097152 | tf_op jit(solution)/shard_map/all_to_all | solution.py:109
  62.1 4.3 copy-start.10
  62.1 19.4 %slice-start = ((s8[16777216]{0:T(1024)(128)(4,1)}), s8[4194304]{0:T(1024)(128)(4,1)S(1)}, s32[]{:S(2)}) async-start(s8[16777216]{0:T(1024)(128)(4,1)} %bitcast.632), calls=%async_computation.1 | async-start | bytes 8388608
  66.4 15.1 %slice-start.1 = ((s8[16777216]{0:T(1024)(128)(4,1)}), s8[4194304]{0:T(1024)(128)(4,1)S(1)}, s32[]{:S(2)}) async-start(s8[16777216]{0:T(1024)(128)(4,1)} %bitcast.632), calls=%async_computation.2 | async-start | bytes 8388608
  66.4 15.1 %slice-start.2 = ((s8[16777216]{0:T(1024)(128)(4,1)}), s8[4194304]{0:T(1024)(128)(4,1)S(1)}, s32[]{:S(2)}) async-start(s8[16777216]{0:T(1024)(128)(4,1)} %bitcast.632), calls=%async_computation.3 | async-start | bytes 8388608
  66.4 15.1 %slice-start.3 = ((s8[16777216]{0:T(1024)(128)(4,1)}), s8[4194304]{0:T(1024)(128)(4,1)S(1)}, s32[]{:S(2)}) async-start(s8[16777216]{0:T(1024)(128)(4,1)} %bitcast.632), calls=%async_computation.4 | async-start | bytes 8388608
  66.4 15.1 %copy-start.9 = (f32[16,128]{1,0:T(8,128)S(1)}, f32[16,128]{1,0:T(8,128)}, u32[]{:S(2)}) copy-start(f32[16,128]{1,0:T(8,128)} %get-tuple-element.1778) | copy-start | bytes 24580
  81.5 6.6 %copy-start.15 = (s32[1,128]{1,0:T(1,128)S(1)}, s32[1,128]{1,0:T(1,128)}, u32[]{:S(2)}) copy-start(s32[1,128]{1,0:T(1,128)} %param.87) | copy-start | bytes 1540
  81.5 7.5 %copy-start.13 = (s32[128]{0:T(128)S(1)}, s32[128]{0:T(128)}, u32[]{:S(2)}) copy-start(s32[128]{0:T(128)} %fusion.21) | copy-start | bytes 1540
  81.5 7.5 %copy-start.1 = (f32[16,16,1,1]{3,0,1,2:T(8,128)S(1)}, f32[16,16,1,1]{3,0,1,2:T(8,128)}, u32[]{:S(2)}) copy-start(f32[16,16,1,1]{3,0,1,2:T(8,128)} %get-tuple-element.1776) | copy-start | bytes 3076
  81.5 7.5 %copy-start.2 = (f32[16,16,1,1]{3,0,1,2:T(8,128)S(1)}, f32[16,16,1,1]{3,0,1,2:T(8,128)}, u32[]{:S(2)}) copy-start(f32[16,16,1,1]{3,0,1,2:T(8,128)} %get-tuple-element.1777) | copy-start | bytes 3076
  81.5 7.5 %copy-start.3 = (f32[1,16,16,1,128]{4,3,2,1,0:T(1,128)S(1)}, f32[1,16,16,1,128]{4,3,2,1,0:T(1,128)}, u32[]{:S(2)}) copy-start(f32[1,16,16,1,128]{4,3,2,1,0:T(1,128)} %get-tuple-element.1770) | copy-start | bytes 393220
  81.5 7.5 %copy-start.4 = (f32[1,16,16,1,128]{4,3,2,1,0:T(1,128)S(1)}, f32[1,16,16,1,128]{4,3,2,1,0:T(1,128)}, u32[]{:S(2)}) copy-start(f32[1,16,16,1,128]{4,3,2,1,0:T(1,128)} %get-tuple-element.1771) | copy-start | bytes 393220
  81.6 7.5 %copy-start.5 = (f32[1,16,16,1,128]{4,3,2,1,0:T(1,128)S(1)}, f32[1,16,16,1,128]{4,3,2,1,0:T(1,128)}, u32[]{:S(2)}) copy-start(f32[1,16,16,1,128]{4,3,2,1,0:T(1,128)} %get-tuple-element.1772) | copy-start | bytes 393220
  81.6 7.5 %copy-start.6 = (f32[1,16,16,1,128]{4,3,2,1,0:T(1,128)S(1)}, f32[1,16,16,1,128]{4,3,2,1,0:T(1,128)}, u32[]{:S(2)}) copy-start(f32[1,16,16,1,128]{4,3,2,1,0:T(1,128)} %get-tuple-element.1773) | copy-start | bytes 393220
  81.6 7.5 %copy-start.7 = (f32[16,16,1,128]{3,2,1,0:T(1,128)S(1)}, f32[16,16,1,128]{3,2,1,0:T(1,128)}, u32[]{:S(2)}) copy-start(f32[16,16,1,128]{3,2,1,0:T(1,128)} %param.82) | copy-start | bytes 393220
  81.6 9.5 %copy-start.12 = (pred[128]{0:T(512)(128)(4,1)S(1)}, pred[128]{0:T(512)(128)(4,1)}, u32[]{:S(2)}) copy-start(pred[128]{0:T(512)(128)(4,1)} %compare_and_fusion) | copy-start | bytes 388
  277.6 4.7 collective-permute-start.2
  555.4 4.6 collective-permute-start.3
  (1 other events, 0.7 us)
